TPU v7x, 32 devices: a whole 2x2x4 slice. The times are simulated.
32 devices in a mesh: band: 2 (over x), grid: 16 (over z, y, core).
Axes of the slice: x: 2, y: 2, z: 4, core: 2. Of those that a mesh axis runs over, the one named last changes fastest.
Arguments:
- start_block: float32 [64, 128, 4, 128], P('band', 'grid'), may hold values from -6 to 6
- previous_block: float32 [64, 128, 4, 128], P('band', 'grid'), may hold values from -6 to 6
- previous_coupling: float32 [64, 64], replicated, may hold values from -0.75 to 0.75
- potential: float32 [128, 4, 128], P('grid'), may hold values from -2 to 2
- atom_cells: int32 [128, 128], P('grid'), may hold values from 0 to 7167, as said below
- atom_proj: float32 [128, 4, 128], P('grid'), may hold values from -1.08 to 1.08
- atom_strength: float32 [128, 4], P('grid'), may hold values from 0.5 to 4
- atom_count: int32 [16], P('grid'), may hold values from 1 to 8, as said below
Outputs:
- a_blocks: float32 [2, 64, 64], P(None, None, 'band')
- b_blocks: float32 [2, 64, 64], P(None, None, 'band')
- final_block: float32 [64, 128, 4, 128], P('band', 'grid')
Inputs may be any that keep to these rules, and one draw needn't show every extreme that they name: `atom_cells`: row a lists 128 distinct cells of atom a's sphere as row-major indices over (14) planes x 4 x 128, counted from the first plane of the slab that holds row a; indices of 4096 or more lie in the first 6 planes of the next slab; on the last slab every index is below 4096. `atom_count`: slots at or past a slab's count are not atoms.
All inputs are finite; a program needn't handle non-finite values.
Results may differ from a plain program's by a relative error of at most 0.0003.
Values sent between devices are 32-bit elements; how exact they have to be, the bound alone decides.
A program may use at most 64 MiB of HBM per device.

v0:
```python
import jax
import jax.numpy as jnp
from jax import lax
from jax.sharding import PartitionSpec as P

NB = 64
STEPS = 2
HIGHEST = lax.Precision.HIGHEST
STENCIL_WEIGHTS = (
    -5369.0 / 1800.0,
    12.0 / 7.0,
    -15.0 / 56.0,
    10.0 / 189.0,
    -1.0 / 112.0,
    2.0 / 1925.0,
    -1.0 / 16632.0,
)


def extended_2(block, sides, width):
    for axis, dim in sides:
        count = lax.axis_size(axis)
        forward = [(i, i + 1) for i in range(count - 1)]
        backward = [(target, source) for source, target in forward]
        low = lax.ppermute(
            lax.slice_in_dim(block, block.shape[dim] - width, None, axis=dim), axis, forward
        )
        high = lax.ppermute(lax.slice_in_dim(block, 0, width, axis=dim), axis, backward)
        block = jnp.concatenate([low, block, high], axis=dim)
    return block


def from_behind(block, axis, distance):
    devices = range(lax.axis_size(axis))
    route = [(i - distance, i) for i in devices if i - distance in devices]
    return lax.ppermute(block, axis, route)


def kinetic_local(haloed, planes):
    center = haloed[:, 6 : 6 + planes]
    width_y, width_z = (center.shape[2], center.shape[3])
    padded = jnp.pad(center, ((0, 0), (0, 0), (6, 6), (6, 6)))
    laplace = 3.0 * STENCIL_WEIGHTS[0] * center
    for k in range(1, 7):
        laplace = laplace + STENCIL_WEIGHTS[k] * (
            haloed[:, 6 + k : 6 + k + planes] + haloed[:, 6 - k : 6 - k + planes]
        )
        laplace = laplace + STENCIL_WEIGHTS[k] * (
            padded[:, :, 6 + k : 6 + k + width_y, 6 : 6 + width_z]
            + padded[:, :, 6 - k : 6 - k + width_y, 6 : 6 + width_z]
        )
        laplace = laplace + STENCIL_WEIGHTS[k] * (
            padded[:, :, 6 : 6 + width_y, 6 + k : 6 + k + width_z]
            + padded[:, :, 6 : 6 + width_y, 6 - k : 6 - k + width_z]
        )
    return -0.5 * laplace


def projector_terms(extended, atom_cells, atom_proj, atom_strength, live_count):
    states_dev = extended.shape[0]
    atom_slots, points = atom_cells.shape
    cell_list = atom_cells.reshape(-1)
    picked = jnp.take(extended, cell_list, axis=1).reshape(states_dev, atom_slots, points)
    coefficient = jnp.einsum("sap,ajp->saj", picked, atom_proj, precision=HIGHEST)
    live_mask = (jnp.arange(atom_slots, dtype=jnp.int32) < live_count).astype(jnp.float32)
    scaled = coefficient * (atom_strength * live_mask[:, None])[None]
    spread = jnp.einsum("saj,ajp->sap", scaled, atom_proj, precision=HIGHEST)
    return jnp.zeros_like(extended).at[:, cell_list].add(spread.reshape(states_dev, -1))


def factor_of(gram):
    factor = jnp.linalg.cholesky(gram)
    identity = jnp.eye(gram.shape[0], dtype=jnp.float32)
    inverse = jax.scipy.linalg.solve_triangular(factor, identity, lower=True)
    return (factor, inverse)


def shards(
    start_block,
    previous_block,
    previous_coupling,
    potential,
    atom_cells,
    atom_proj,
    atom_strength,
    atom_count,
):
    states_dev, planes, width_y, width_z = start_block.shape
    cell_total = planes * lax.axis_size("grid") * width_y * width_z
    offset = lax.axis_index("band") * states_dev
    live_count = atom_count[0]
    a_list = []
    b_list = []

    def to_cells(block):
        return lax.all_to_all(block, "band", split_axis=1, concat_axis=0, tiled=True)

    def to_states(block):
        return lax.all_to_all(block, "band", split_axis=0, concat_axis=1, tiled=True)

    def summed(matrix):
        return lax.psum(matrix, ("band", "grid"))

    start_cells = to_cells(start_block)
    cell_shape = start_cells.shape
    start_flat = start_cells.reshape(NB, -1)
    factor, inverse = factor_of(
        summed(jnp.dot(start_flat, start_flat.T, precision=HIGHEST) / cell_total)
    )
    current_cells = jnp.dot(inverse, start_flat, precision=HIGHEST)
    previous_cells = to_cells(previous_block).reshape(NB, -1)
    coupling = previous_coupling
    current_local = to_states(current_cells.reshape(cell_shape))
    for iteration in range(STEPS):
        haloed = extended_2(current_local, (("grid", 1),), 6)
        kinetic_part = kinetic_local(haloed, planes)
        extended = haloed[:, 6:].reshape(states_dev, -1)
        terms = projector_terms(extended, atom_cells, atom_proj, atom_strength, live_count)
        terms = terms.reshape(states_dev, planes + 6, width_y, width_z)
        received = from_behind(terms[:, planes:], "grid", 1)
        own_terms = terms[:, :planes].at[:, :6].add(received)
        applied = kinetic_part + potential[None] * current_local + own_terms
        applied_cells = to_cells(applied).reshape(NB, -1)
        correlation = summed(
            jnp.dot(current_cells, applied_cells.T, precision=HIGHEST) / cell_total
        )
        residual_block = (
            applied_cells
            - jnp.dot(correlation.T, current_cells, precision=HIGHEST)
            - jnp.dot(coupling, previous_cells, precision=HIGHEST)
        )
        factor, inverse = factor_of(
            summed(jnp.dot(residual_block, residual_block.T, precision=HIGHEST) / cell_total)
        )
        coupling = factor.T
        a_list.append(lax.dynamic_slice_in_dim(correlation, offset, states_dev, 1))
        b_list.append(lax.dynamic_slice_in_dim(coupling, offset, states_dev, 1))
        previous_cells = current_cells
        current_cells = jnp.dot(inverse, residual_block, precision=HIGHEST)
        current_local = to_states(current_cells.reshape(cell_shape))
    return (jnp.stack(a_list), jnp.stack(b_list), current_local)


def solution(mesh):
    in_specs = (
        P("band", "grid", None, None),
        P("band", "grid", None, None),
        P(),
        P("grid", None, None),
        P("grid", None),
        P("grid", None, None),
        P("grid", None),
        P("grid"),
    )
    out_specs = (P(None, None, "band"), P(None, None, "band"), P("band", "grid", None, None))
    return jax.shard_map(shards, mesh=mesh, in_specs=in_specs, out_specs=out_specs, check_vma=False)
```

profile of v0, /device:TPU:0, one launch (start us, length us, event | category | flops | bytes accessed | tf_op | source)
XLA Modules:
  0.0 424.2 jit_solution(2157985983389813124)
XLA Ops:
  0.6 1.9 copy.51
  2.6 4.3 %all-to-all-start = ((f32[32,8,4,128]{3,2,0,1:T(4,128)}), f32[32,8,4,128]{3,2,0,1:T(4,128)S(1)}, u32[]{:S(2)}, u32[]{:S(2)}) async-start(f32[32,8,4,128]{3,2,0,1:T(4,128)} %copy.51), calls=%async_computation | async-start | bytes 1048576 | tf_op jit(solution)/shard_map/all_to_all | solution.py:96
  7.6 8.1 %all-to-all-done = f32[32,8,4,128]{3,2,0,1:T(4,128)S(1)} async-done(((f32[32,8,4,128]{3,2,0,1:T(4,128)}), f32[32,8,4,128]{3,2,0,1:T(4,128)S(1)}, u32[]{:S(2)}, u32[]{:S(2)}) %all-to-all-start) | async-done | bytes 524320 | tf_op jit(solution)/shard_map/all_to_all | solution.py:96
  16.5 40.0 %psum.35 = f32[64,64]{0,1:T(8,128)S(1)} all-reduce(f32[64,64]{0,1:T(8,128)S(1)} %convolution_multiply_fusion.4), channel_id=1, replica_groups=mesh['band'=2,'grid'=16] {'band','grid'}, use_global_device_ids=true, to_apply=%region_0.0 | all-reduce | flops 4096 | bytes 32768 | tf_op jit(solution)/shard_map/psum | solution.py:102
  56.6 5.8 %cholesky.59 = f32[64,64]{1,0:T(8,128)S(1)} custom-call(f32[64,64]{1,0:T(8,128)S(1)} %fusion.140), custom_call_target="Cholesky" | custom-call | tf_op jit(solution)/shard_map/jit(cholesky)/cholesky | solution.py:72
  63.8 4.9 %custom-call.7 = f32[1,64,64]{1,2,0:T(8,128)S(1)} custom-call(f32[1,64,64]{2,1,0:T(8,128)S(1)} %fusion.134), custom_call_target="InvertDiagBlocksLowerTriangular" | custom-call | tf_op jit(solution)/shard_map/jit(_solve_triangular)/triangular_solve | solution.py:74
  70.7 3.5 all-to-all-start.1
  74.3 7.9 %all-to-all-done.1 = f32[64,4,4,128]{3,2,1,0:T(4,128)S(1)} async-done(((f32[64,4,4,128]{3,2,1,0:T(4,128)}), f32[64,4,4,128]{3,2,1,0:T(4,128)S(1)}, u32[]{:S(2)}, u32[]{:S(2)}) %all-to-all-start.1) | async-done | bytes 524320 | tf_op jit(solution)/shard_map/all_to_all | solution.py:99
  84.5 2.3 collective-permute-done
  87.6 2.4 copy.56
  90.1 4.8 %gather_fusion = f32[1024,32]{1,0:T(8,128)S(1)} fusion(f32[32,7168]{0,1:T(8,128)} %bitcast.150, s32[1024]{0:T(1024)S(1)} %fusion.141), kind=kCustom, calls=%fused_computation.clone | custom fusion | bytes 266240 | tf_op jit(solution)/shard_map/jit(_take)/gather | solution.py:63
  96.3 8.0 %scatter_custom_fusion = f32[32,7168]{0,1:T(8,128)} fusion(s32[1024]{0:T(1024)S(1)} %bitcast.165, f32[1024,32]{1,0:T(8,128)S(1)} %copy.60, f32[]{:T(128)} %constant.127.clone.1), kind=kCustom, calls=%fused_computation.60 | custom fusion | flops 32768 | bytes 917508 | tf_op jit(solution)/shard_map/scatter-add | solution.py:68
  104.3 3.4 fusion.143
  108.9 8.3 %collective-permute-start.2 = (f32[32,6,4,128]{3,0,2,1:T(8,128)}, f32[32,6,4,128]{3,0,2,1:T(8,128)}, u32[]{:S(2)}, u32[]{:S(2)}) collective-permute-start(f32[32,6,4,128]{3,0,2,1:T(8,128)} %copy.92), channel_id=1, source_target_pairs={{0,1},{1,2},{2,3},{3,4},{4,5},{5,6},{6,7},{7,8},{8,9},{9,10},{10,1... | collective-permute-start | bytes 1179656 | tf_op jit(solution)/shard_map/ppermute | solution.py:36
  117.2 2.0 collective-permute-start.1
  120.2 4.2 all-to-all-start.3
  124.4 1.7 slice.410
  126.1 2.6 copy.91
  128.7 1.4 copy.90
  130.1 1.9 add_dynamic-update-slice_fusion.1
  132.0 4.3 %fusion.51 = f32[32,8,4,128]{3,0,2,1:T(8,128)} fusion(f32[32,8,4,128]{3,0,2,1:T(8,128)} %add_dynamic-update-slice_fusion.1, f32[32,8,4,128]{3,0,2,1:T(8,128)S(1)} %bitcast.145, f32[32,6,4,128]{3,0,2,1:T(8,128)} %collective-permute-done.1, f32[32,6,4,128]{3,0,2,1:T(8,128)} %copy-done.3, f32[8,4,128]{2,1,0:T(4,128)S(1)} %copy-done.7), kind=kLoop, calls=%fused_computation.150 | loop fusion | flops 8388608 | bytes 2375680 | tf_op jit(solution)/shard_map/add | solution.py:122
  136.4 3.7 all-to-all-start.2
  141.4 7.5 %all-to-all-done.2 = f32[32,8,4,128]{3,0,2,1:T(8,128)S(1)} async-done(((f32[32,8,4,128]{3,0,2,1:T(8,128)}), f32[32,8,4,128]{3,0,2,1:T(8,128)S(1)}, u32[]{:S(2)}, u32[]{:S(2)}) %all-to-all-start.2) | async-done | bytes 524320 | tf_op jit(solution)/shard_map/all_to_all | solution.py:96
  150.0 38.9 %psum.36 = f32[64,64]{0,1:T(8,128)S(1)} all-reduce(f32[64,64]{0,1:T(8,128)S(1)} %convolution_multiply_fusion.3), channel_id=1, replica_groups=mesh['band'=2,'grid'=16] {'band','grid'}, use_global_device_ids=true, to_apply=%region_4.8 | all-reduce | flops 4096 | bytes 32768 | tf_op jit(solution)/shard_map/psum | solution.py:102
  190.7 39.4 %psum.37 = f32[64,64]{0,1:T(8,128)S(1)} all-reduce(f32[64,64]{0,1:T(8,128)S(1)} %convolution_multiply_fusion.2), channel_id=1, replica_groups=mesh['band'=2,'grid'=16] {'band','grid'}, use_global_device_ids=true, to_apply=%region_5.9 | all-reduce | flops 4096 | bytes 32768 | tf_op jit(solution)/shard_map/psum | solution.py:102
  230.2 5.8 %cholesky.70 = f32[64,64]{1,0:T(8,128)S(1)} custom-call(f32[64,64]{1,0:T(8,128)S(1)} %fusion.138), custom_call_target="Cholesky" | custom-call | tf_op jit(solution)/shard_map/jit(cholesky)/cholesky | solution.py:72
  237.4 4.9 %custom-call.8 = f32[1,64,64]{1,2,0:T(8,128)S(1)} custom-call(f32[1,64,64]{2,1,0:T(8,128)S(1)} %get-tuple-element.32), custom_call_target="InvertDiagBlocksLowerTriangular" | custom-call | tf_op jit(solution)/shard_map/jit(_solve_triangular)/triangular_solve | solution.py:74
  243.5 10.8 %all_to_all.114 = f32[64,4,4,128]{3,2,1,0:T(4,128)S(1)} all-to-all(f32[64,4,4,128]{3,2,1,0:T(4,128)S(1)} %reshape.189), channel_id=1, replica_groups=mesh['band'=2,'grid'=16] {'band'}, dimensions={0} | all-to-all | bytes 1048576 | tf_op jit(solution)/shard_map/all_to_all | solution.py:99
  256.6 2.3 collective-permute-done.3
  259.7 2.4 copy.71
  262.1 4.8 %gather_fusion.1 = f32[1024,32]{1,0:T(8,128)S(1)} fusion(f32[32,7168]{0,1:T(8,128)} %bitcast.149, s32[1024]{0:T(1024)S(1)} %fusion.141), kind=kCustom, calls=%fused_computation.1.clone | custom fusion | bytes 266240 | tf_op jit(solution)/shard_map/jit(_take)/gather | solution.py:63
  268.4 8.0 %scatter_custom_fusion.1 = f32[32,7168]{0,1:T(8,128)} fusion(s32[1024]{0:T(1024)S(1)} %bitcast.166, f32[1024,32]{1,0:T(8,128)S(1)} %copy.74, f32[]{:T(128)} %constant.127.clone.1), kind=kCustom, calls=%fused_computation.58 | custom fusion | flops 32768 | bytes 917508 | tf_op jit(solution)/shard_map/scatter-add | solution.py:68
  276.4 3.3 fusion.142
  280.9 8.4 %collective-permute-start.5 = (f32[32,6,4,128]{3,0,2,1:T(8,128)}, f32[32,6,4,128]{3,0,2,1:T(8,128)}, u32[]{:S(2)}, u32[]{:S(2)}) collective-permute-start(f32[32,6,4,128]{3,0,2,1:T(8,128)} %copy.95), channel_id=1, source_target_pairs={{0,1},{1,2},{2,3},{3,4},{4,5},{5,6},{6,7},{7,8},{8,9},{9,10},{10,1... | collective-permute-start | bytes 1179656 | tf_op jit(solution)/shard_map/ppermute | solution.py:36
  289.3 2.0 collective-permute-start.4
  291.4 1.7 slice.437
  293.1 2.6 copy.94
  295.7 1.4 copy.93
  297.1 2.0 add_dynamic-update-slice_fusion
  299.0 4.5 %fusion.16 = f32[32,8,4,128]{3,0,2,1:T(8,128)} fusion(f32[32,8,4,128]{3,0,2,1:T(8,128)} %add_dynamic-update-slice_fusion, f32[32,8,4,128]{3,0,2,1:T(8,128)S(1)} %bitcast.148, f32[32,6,4,128]{3,0,2,1:T(8,128)} %collective-permute-done.4, f32[32,6,4,128]{3,0,2,1:T(8,128)} %copy-done.4, f32[8,4,128]{2,1,0:T(4,128)S(1)} %copy-done.7), kind=kLoop, calls=%fused_computation.115 | loop fusion | flops 8388608 | bytes 2375680 | tf_op jit(solution)/shard_map/add | solution.py:122
  303.5 3.5 all-to-all-start.5
  307.1 8.5 %all-to-all-done.5 = f32[32,8,4,128]{3,0,2,1:T(8,128)S(1)} async-done(((f32[32,8,4,128]{3,0,2,1:T(8,128)}), f32[32,8,4,128]{3,0,2,1:T(8,128)S(1)}, u32[]{:S(2)}, u32[]{:S(2)}) %all-to-all-start.5) | async-done | bytes 524320 | tf_op jit(solution)/shard_map/all_to_all | solution.py:96
  316.7 39.2 %psum.38 = f32[64,64]{0,1:T(8,128)S(1)} all-reduce(f32[64,64]{0,1:T(8,128)S(1)} %convolution_multiply_fusion.1), channel_id=1, replica_groups=mesh['band'=2,'grid'=16] {'band','grid'}, use_global_device_ids=true, to_apply=%region_7.11 | all-reduce | flops 4096 | bytes 32768 | tf_op jit(solution)/shard_map/psum | solution.py:102
  357.8 40.5 %psum.39 = f32[64,64]{0,1:T(8,128)S(1)} all-reduce(f32[64,64]{0,1:T(8,128)S(1)} %convolution_multiply_fusion), channel_id=1, replica_groups=mesh['band'=2,'grid'=16] {'band','grid'}, use_global_device_ids=true, to_apply=%region_8.12 | all-reduce | flops 4096 | bytes 32768 | tf_op jit(solution)/shard_map/psum | solution.py:102
  398.3 5.8 %cholesky.81 = f32[64,64]{1,0:T(8,128)S(1)} custom-call(f32[64,64]{1,0:T(8,128)S(1)} %fusion.136), custom_call_target="Cholesky" | custom-call | tf_op jit(solution)/shard_map/jit(cholesky)/cholesky | solution.py:72
  405.5 4.9 %custom-call.9 = f32[1,64,64]{1,2,0:T(8,128)S(1)} custom-call(f32[1,64,64]{2,1,0:T(8,128)S(1)} %get-tuple-element.30), custom_call_target="InvertDiagBlocksLowerTriangular" | custom-call | tf_op jit(solution)/shard_map/jit(_solve_triangular)/triangular_solve | solution.py:74
  412.4 3.5 all-to-all-start.6
  417.2 6.2 %all-to-all-done.6 = f32[64,4,4,128]{3,2,1,0:T(4,128)S(1)} async-done(((f32[64,4,4,128]{3,2,1,0:T(4,128)}), f32[64,4,4,128]{3,2,1,0:T(4,128)S(1)}, u32[]{:S(2)}, u32[]{:S(2)}) %all-to-all-start.6) | async-done | bytes 524320 | tf_op jit(solution)/shard_map/all_to_all | solution.py:99
  (100 shorter events, 31.8 us)
Async XLA Ops:
  0.6 188.9 %copy-start = (f32[64,64]{1,0:T(8,128)S(1)}, f32[64,64]{1,0:T(8,128)}, u32[]{:S(2)}) copy-start(f32[64,64]{1,0:T(8,128)} %param.19) | copy-start | bytes 49156
  2.6 71.6 %copy-start.9 = (f32[8,4]{0,1:T(4,128)S(1)}, f32[8,4]{0,1:T(4,128)}, u32[]{:S(2)}) copy-start(f32[8,4]{0,1:T(4,128)} %param.23) | copy-start | bytes 388
  2.6 71.7 %copy-start.8 = (s32[8,128]{1,0:T(8,128)S(1)}, s32[8,128]{1,0:T(8,128)}, u32[]{:S(2)}) copy-start(s32[8,128]{1,0:T(8,128)} %param.21) | copy-start | bytes 12292
  2.6 13.1 %all-to-all-start = ((f32[32,8,4,128]{3,2,0,1:T(4,128)}), f32[32,8,4,128]{3,2,0,1:T(4,128)S(1)}, u32[]{:S(2)}, u32[]{:S(2)}) async-start(f32[32,8,4,128]{3,2,0,1:T(4,128)} %copy.51), calls=%async_computation | async-start | bytes 1048576 | tf_op jit(solution)/shard_map/all_to_all | solution.py:96
  70.7 11.5 %all-to-all-start.1 = ((f32[64,4,4,128]{3,2,1,0:T(4,128)}), f32[64,4,4,128]{3,2,1,0:T(4,128)S(1)}, u32[]{:S(2)}, u32[]{:S(2)}) async-start(f32[64,4,4,128]{3,2,1,0:T(4,128)} %reshape.180), calls=%async_computation.1 | async-start | bytes 1048576 | tf_op jit(solution)/shard_map/all_to_all | solution.py:99
  83.2 3.6 collective-permute-start
  86.8 0.8 copy-start.3
  87.6 7.5 %copy-start.6 = (f32[8,4,128]{2,1,0:T(4,128)S(1)}, f32[8,4,128]{2,1,0:T(4,128)}, u32[]{:S(2)}) copy-start(f32[8,4,128]{2,1,0:T(4,128)} %param.22) | copy-start | bytes 49156
  104.3 14.9 %copy-start.5 = (f32[32,8,4,128]{3,2,1,0:T(4,128)S(1)}, f32[32,8,4,128]{3,2,1,0:T(4,128)}, u32[]{:S(2)}) copy-start(f32[32,8,4,128]{3,2,1,0:T(4,128)} %param.18) | copy-start | bytes 1572868
  108.9 21.2 %collective-permute-start.2 = (f32[32,6,4,128]{3,0,2,1:T(8,128)}, f32[32,6,4,128]{3,0,2,1:T(8,128)}, u32[]{:S(2)}, u32[]{:S(2)}) collective-permute-start(f32[32,6,4,128]{3,0,2,1:T(8,128)} %copy.92), channel_id=1, source_target_pairs={{0,1},{1,2},{2,3},{3,4},{4,5},{5,6},{6,7},{7,8},{8,9},{9,10},{10,1... | collective-permute-start | bytes 1179656 | tf_op jit(solution)/shard_map/ppermute | solution.py:36
  117.2 14.8 %collective-permute-start.1 = (f32[32,6,4,128]{3,0,2,1:T(8,128)}, f32[32,6,4,128]{3,0,2,1:T(8,128)}, u32[]{:S(2)}, u32[]{:S(2)}) collective-permute-start(f32[32,6,4,128]{3,0,2,1:T(8,128)} %get-tuple-element.40), channel_id=1, source_target_pairs={{0,1},{1,2},{2,3},{3,4},{4,5},{5,6},{6,7},{7,8},{8,9},{9,10},{10,1... | collective-permute-start | bytes 1179656 | tf_op jit(solution)/shard_map/ppermute | solution.py:25
  120.2 16.2 %all-to-all-start.3 = ((f32[32,8,4,128]{3,2,0,1:T(4,128)}), f32[32,8,4,128]{3,2,0,1:T(4,128)}, u32[]{:S(2)}, u32[]{:S(2)}) async-start(f32[32,8,4,128]{3,2,0,1:T(4,128)} %copy.66), calls=%async_computation.3 | async-start | bytes 1048576 | tf_op jit(solution)/shard_map/all_to_all | solution.py:96
  126.1 5.9 %copy-start.7 = (f32[8,4,128]{2,1,0:T(4,128)S(1)}, f32[8,4,128]{2,1,0:T(4,128)}, u32[]{:S(2)}) copy-start(f32[8,4,128]{2,1,0:T(4,128)} %param.20) | copy-start | bytes 49156
  136.4 12.5 %all-to-all-start.2 = ((f32[32,8,4,128]{3,0,2,1:T(8,128)}), f32[32,8,4,128]{3,0,2,1:T(8,128)S(1)}, u32[]{:S(2)}, u32[]{:S(2)}) async-start(f32[32,8,4,128]{3,0,2,1:T(8,128)} %fusion.51), calls=%async_computation.2 | async-start | bytes 1048576 | tf_op jit(solution)/shard_map/all_to_all | solution.py:96
  243.1 11.1 %copy-start.1 = (f32[64,2048]{1,0:T(8,128)}, f32[64,2048]{1,0:T(8,128)S(1)}, u32[]{:S(2)}) copy-start(f32[64,2048]{1,0:T(8,128)S(1)} %fusion.147) | copy-start | bytes 1572868
  255.3 3.6 collective-permute-start.3
  258.9 0.7 copy-start.4
  280.9 16.2 %collective-permute-start.5 = (f32[32,6,4,128]{3,0,2,1:T(8,128)}, f32[32,6,4,128]{3,0,2,1:T(8,128)}, u32[]{:S(2)}, u32[]{:S(2)}) collective-permute-start(f32[32,6,4,128]{3,0,2,1:T(8,128)} %copy.95), channel_id=1, source_target_pairs={{0,1},{1,2},{2,3},{3,4},{4,5},{5,6},{6,7},{7,8},{8,9},{9,10},{10,1... | collective-permute-start | bytes 1179656 | tf_op jit(solution)/shard_map/ppermute | solution.py:36
  289.3 9.7 %collective-permute-start.4 = (f32[32,6,4,128]{3,0,2,1:T(8,128)}, f32[32,6,4,128]{3,0,2,1:T(8,128)}, u32[]{:S(2)}, u32[]{:S(2)}) collective-permute-start(f32[32,6,4,128]{3,0,2,1:T(8,128)} %get-tuple-element.38), channel_id=1, source_target_pairs={{0,1},{1,2},{2,3},{3,4},{4,5},{5,6},{6,7},{7,8},{8,9},{9,10},{10,1... | collective-permute-start | bytes 1179656 | tf_op jit(solution)/shard_map/ppermute | solution.py:25
  297.1 19.1 %copy-start.2 = (f32[64,2048]{1,0:T(8,128)S(1)}, f32[64,2048]{1,0:T(8,128)}, u32[]{:S(2)}) copy-start(f32[64,2048]{1,0:T(8,128)} %copy-done.1) | copy-start | bytes 1572868
  303.5 12.0 %all-to-all-start.5 = ((f32[32,8,4,128]{3,0,2,1:T(8,128)}), f32[32,8,4,128]{3,0,2,1:T(8,128)S(1)}, u32[]{:S(2)}, u32[]{:S(2)}) async-start(f32[32,8,4,128]{3,0,2,1:T(8,128)} %fusion.16), calls=%async_computation.5 | async-start | bytes 1048576 | tf_op jit(solution)/shard_map/all_to_all | solution.py:96
  412.4 11.0 %all-to-all-start.6 = ((f32[64,4,4,128]{3,2,1,0:T(4,128)}), f32[64,4,4,128]{3,2,1,0:T(4,128)S(1)}, u32[]{:S(2)}, u32[]{:S(2)}) async-start(f32[64,4,4,128]{3,2,1,0:T(4,128)} %reshape.195), calls=%async_computation.6 | async-start | bytes 1048576 | tf_op jit(solution)/shard_map/all_to_all | solution.py:99
where the time goes:
time: 426 us; the launch traced here: 424 us
  blocking collectives  209 us (49%)
  other arithmetic  66.8 us (16%)
  local copies, waits for them, and re-layouts  48.4 us (11%)
  starting transfers between devices  46.1 us (11%)
  waiting for transfers between devices  42.7 us (10%)
  matrix products  9.6 us (2%)
    psum x5, blocking collectives, summed(): return lax.psum(matrix, ('band', 'grid'))  198 us
    all_to_all x4, waiting for transfers between devices, to_cells(): lax.all_to_all(block, 'band', split_axis=1, concat_axis=0, tiled=True)  24 us
    another operation x9, other arithmetic, factor_of(): factor = jnp.linalg.cholesky(gram)  19.6 us
    ppermute x2, starting transfers between devices, from_behind(): return lax.ppermute(block, axis, route)  16.7 us
    another operation x6, other arithmetic, factor_of(): inverse = jax.scipy.linalg.solve_triangular(factor, identity, lower=True)  16.6 us
    scatter-add x2, other arithmetic, projector_terms(): jnp.zeros_like(extended).at[:, cell_list]  16 us
    all_to_all x4, starting transfers between devices, to_cells(): lax.all_to_all(block, 'band', split_axis=1, concat_axis=0, tiled=True)  15.7 us
    unnamed x28, local copies, waits for them, and re-layouts  14.7 us
  transfers between devices with their start and end apart: 12, of which 7 were waited for; matrix products, arithmetic and copies ran while one was open for 5% of the time, Pallas kernels for 0%

commit v1 on v0

--- a/solution.py
+++ b/solution.py
@@ -99,7 +99,7 @@
         return lax.all_to_all(block, "band", split_axis=0, concat_axis=1, tiled=True)
 
     def summed(matrix):
-        return lax.psum(matrix, ("band", "grid"))
+        return lax.psum(lax.psum(matrix, "grid"), "band")
 
     start_cells = to_cells(start_block)
     cell_shape = start_cells.shape

time: 426 us -> 542 us (1.27)
  blocking collectives: 209 us -> 339 us
  starting transfers between devices: 46.1 us -> 36.4 us
    psum x5 -> x10, blocking collectives: 198 us -> 330 us  [summed(): return lax.psum(lax.psum(matrix, 'grid'), 'band')]
    ppermute x2, starting transfers between devices: 16.7 us -> 7.16 us  [from_behind(): return lax.ppermute(block, axis, route)]
  transfers between devices with their start and end apart: 12 -> 12, of which waited for: 7 -> 7; matrix products, arithmetic and copies ran while one was open for 5% -> 4% of each run, Pallas kernels for 0% -> 0%
where the time goes in v1:
time: 542 us; the launch traced here: 541 us
  blocking collectives  339 us (63%)
  other arithmetic  66.8 us (12%)
  local copies, waits for them, and re-layouts  48.4 us (9%)
  waiting for transfers between devices  38.4 us (7%)
  starting transfers between devices  36.4 us (7%)
  matrix products  9.6 us (2%)
    psum x10, blocking collectives, summed(): return lax.psum(lax.psum(matrix, 'grid'), 'band')  330 us
    all_to_all x4, waiting for transfers between devices, to_cells(): lax.all_to_all(block, 'band', split_axis=1, concat_axis=0, tiled=True)  22 us
    another operation x9, other arithmetic, factor_of(): factor = jnp.linalg.cholesky(gram)  19.6 us
    another operation x6, other arithmetic, factor_of(): inverse = jax.scipy.linalg.solve_triangular(factor, identity, lower=True)  16.6 us
    scatter-add x2, other arithmetic, projector_terms(): jnp.zeros_like(extended).at[:, cell_list]  16 us
    all_to_all x4, starting transfers between devices, to_cells(): lax.all_to_all(block, 'band', split_axis=1, concat_axis=0, tiled=True)  15.6 us
    unnamed x28, local copies, waits for them, and re-layouts  14.7 us
    all_to_all x2, waiting for transfers between devices, to_states(): lax.all_to_all(block, 'band', split_axis=0, concat_axis=1, tiled=True)  11.8 us
  transfers between devices with their start and end apart: 12, of which 7 were waited for; matrix products, arithmetic and copies ran while one was open for 4% of the time, Pallas kernels for 0%

profile of v1, /device:TPU:0, one launch (start us, length us, event | category | flops | bytes accessed | tf_op | source)
XLA Modules:
  0.0 540.7 jit_solution(10470912795134010523)
XLA Ops:
  0.6 1.9 copy.51
  2.6 4.2 all-to-all-start
  7.5 8.0 %all-to-all-done = f32[32,8,4,128]{3,2,0,1:T(4,128)S(1)} async-done(((f32[32,8,4,128]{3,2,0,1:T(4,128)}), f32[32,8,4,128]{3,2,0,1:T(4,128)S(1)}, u32[]{:S(2)}, u32[]{:S(2)}) %all-to-all-start) | async-done | bytes 524320 | tf_op jit(solution)/shard_map/all_to_all | solution.py:96
  16.4 60.9 %psum.70 = f32[64,64]{0,1:T(8,128)S(1)} all-reduce(f32[64,64]{0,1:T(8,128)S(1)} %convolution_multiply_fusion.4), channel_id=1, replica_groups=mesh['band'=2,'grid'=16] {'grid'}, use_global_device_ids=true, to_apply=%region_0.0 | all-reduce | flops 4096 | bytes 32768 | tf_op jit(solution)/shard_map/psum | solution.py:102
  77.3 7.5 %psum.71 = f32[64,64]{0,1:T(8,128)S(1)} all-reduce(f32[64,64]{0,1:T(8,128)S(1)} %psum.70), channel_id=1, replica_groups=mesh['band'=2,'grid'=16] {'band'}, use_global_device_ids=true, to_apply=%region_1.0 | all-reduce | flops 4096 | bytes 32768 | tf_op jit(solution)/shard_map/psum | solution.py:102
  84.8 5.8 %cholesky.59 = f32[64,64]{1,0:T(8,128)S(1)} custom-call(f32[64,64]{1,0:T(8,128)S(1)} %fusion.140), custom_call_target="Cholesky" | custom-call | tf_op jit(solution)/shard_map/jit(cholesky)/cholesky | solution.py:72
  92.0 4.9 custom-call.7
  98.9 3.5 all-to-all-start.1
  102.5 6.5 %all-to-all-done.1 = f32[64,4,4,128]{3,2,1,0:T(4,128)S(1)} async-done(((f32[64,4,4,128]{3,2,1,0:T(4,128)}), f32[64,4,4,128]{3,2,1,0:T(4,128)S(1)}, u32[]{:S(2)}, u32[]{:S(2)}) %all-to-all-start.1) | async-done | bytes 524320 | tf_op jit(solution)/shard_map/all_to_all | solution.py:99
  111.3 2.3 collective-permute-done
  114.4 2.4 copy.56
  116.8 4.8 gather_fusion
  123.1 8.0 %scatter_custom_fusion = f32[32,7168]{0,1:T(8,128)} fusion(s32[1024]{0:T(1024)S(1)} %bitcast.165, f32[1024,32]{1,0:T(8,128)S(1)} %copy.60, f32[]{:T(128)} %constant.127.clone.1), kind=kCustom, calls=%fused_computation.60 | custom fusion | flops 32768 | bytes 917508 | tf_op jit(solution)/shard_map/scatter-add | solution.py:68
  131.1 3.4 fusion.143
  135.7 3.6 collective-permute-start.2
  139.3 2.0 collective-permute-start.1
  142.2 4.2 all-to-all-start.3
  148.2 2.6 copy.91
  154.1 4.3 fusion.51
  158.4 3.7 all-to-all-start.2
  163.5 6.2 %all-to-all-done.2 = f32[32,8,4,128]{3,0,2,1:T(8,128)S(1)} async-done(((f32[32,8,4,128]{3,0,2,1:T(8,128)}), f32[32,8,4,128]{3,0,2,1:T(8,128)S(1)}, u32[]{:S(2)}, u32[]{:S(2)}) %all-to-all-start.2) | async-done | bytes 524320 | tf_op jit(solution)/shard_map/all_to_all | solution.py:96
  170.8 57.6 %psum.72 = f32[64,64]{0,1:T(8,128)S(1)} all-reduce(f32[64,64]{0,1:T(8,128)S(1)} %convolution_multiply_fusion.3), channel_id=1, replica_groups=mesh['band'=2,'grid'=16] {'grid'}, use_global_device_ids=true, to_apply=%region_5.9 | all-reduce | flops 4096 | bytes 32768 | tf_op jit(solution)/shard_map/psum | solution.py:102
  228.5 7.2 %psum.73 = f32[64,64]{0,1:T(8,128)S(1)} all-reduce(f32[64,64]{0,1:T(8,128)S(1)} %psum.72), channel_id=1, replica_groups=mesh['band'=2,'grid'=16] {'band'}, use_global_device_ids=true, to_apply=%region_6.10 | all-reduce | flops 4096 | bytes 32768 | tf_op jit(solution)/shard_map/psum | solution.py:102
  237.4 57.6 %psum.74 = f32[64,64]{0,1:T(8,128)S(1)} all-reduce(f32[64,64]{0,1:T(8,128)S(1)} %convolution_multiply_fusion.2), channel_id=1, replica_groups=mesh['band'=2,'grid'=16] {'grid'}, use_global_device_ids=true, to_apply=%region_7.11 | all-reduce | flops 4096 | bytes 32768 | tf_op jit(solution)/shard_map/psum | solution.py:102
  295.0 8.6 %psum.75 = f32[64,64]{0,1:T(8,128)S(1)} all-reduce(f32[64,64]{0,1:T(8,128)S(1)} %psum.74), channel_id=1, replica_groups=mesh['band'=2,'grid'=16] {'band'}, use_global_device_ids=true, to_apply=%region_8.12 | all-reduce | flops 4096 | bytes 32768 | tf_op jit(solution)/shard_map/psum | solution.py:102
  303.7 5.8 %cholesky.70 = f32[64,64]{1,0:T(8,128)S(1)} custom-call(f32[64,64]{1,0:T(8,128)S(1)} %fusion.138), custom_call_target="Cholesky" | custom-call | tf_op jit(solution)/shard_map/jit(cholesky)/cholesky | solution.py:72
  310.8 4.9 custom-call.8
  316.9 9.0 %all_to_all.114 = f32[64,4,4,128]{3,2,1,0:T(4,128)S(1)} all-to-all(f32[64,4,4,128]{3,2,1,0:T(4,128)S(1)} %reshape.189), channel_id=1, replica_groups=mesh['band'=2,'grid'=16] {'band'}, dimensions={0} | all-to-all | bytes 1048576 | tf_op jit(solution)/shard_map/all_to_all | solution.py:99
  328.2 2.3 collective-permute-done.3
  331.3 2.4 copy.71
  333.8 4.8 gather_fusion.1
  340.0 8.0 %scatter_custom_fusion.1 = f32[32,7168]{0,1:T(8,128)} fusion(s32[1024]{0:T(1024)S(1)} %bitcast.166, f32[1024,32]{1,0:T(8,128)S(1)} %copy.74, f32[]{:T(128)} %constant.127.clone.1), kind=kCustom, calls=%fused_computation.58 | custom fusion | flops 32768 | bytes 917508 | tf_op jit(solution)/shard_map/scatter-add | solution.py:68
  348.0 3.3 fusion.142
  352.6 3.6 collective-permute-start.5
  356.2 2.0 collective-permute-start.4
  359.9 2.6 copy.94
  363.9 2.0 add_dynamic-update-slice_fusion
  365.9 4.5 fusion.16
  370.4 3.5 all-to-all-start.5
  373.9 7.8 %all-to-all-done.5 = f32[32,8,4,128]{3,0,2,1:T(8,128)S(1)} async-done(((f32[32,8,4,128]{3,0,2,1:T(8,128)}), f32[32,8,4,128]{3,0,2,1:T(8,128)S(1)}, u32[]{:S(2)}, u32[]{:S(2)}) %all-to-all-start.5) | async-done | bytes 524320 | tf_op jit(solution)/shard_map/all_to_all | solution.py:96
  382.8 57.6 %psum.76 = f32[64,64]{0,1:T(8,128)S(1)} all-reduce(f32[64,64]{0,1:T(8,128)S(1)} %convolution_multiply_fusion.1), channel_id=1, replica_groups=mesh['band'=2,'grid'=16] {'grid'}, use_global_device_ids=true, to_apply=%region_10.14 | all-reduce | flops 4096 | bytes 32768 | tf_op jit(solution)/shard_map/psum | solution.py:102
  440.5 7.1 %psum.77 = f32[64,64]{0,1:T(8,128)S(1)} all-reduce(f32[64,64]{0,1:T(8,128)S(1)} %psum.76), channel_id=1, replica_groups=mesh['band'=2,'grid'=16] {'band'}, use_global_device_ids=true, to_apply=%region_11.15 | all-reduce | flops 4096 | bytes 32768 | tf_op jit(solution)/shard_map/psum | solution.py:102
  449.4 57.6 %psum.78 = f32[64,64]{0,1:T(8,128)S(1)} all-reduce(f32[64,64]{0,1:T(8,128)S(1)} %convolution_multiply_fusion), channel_id=1, replica_groups=mesh['band'=2,'grid'=16] {'grid'}, use_global_device_ids=true, to_apply=%region_12.16 | all-reduce | flops 4096 | bytes 32768 | tf_op jit(solution)/shard_map/psum | solution.py:102
  507.0 8.6 %psum.79 = f32[64,64]{0,1:T(8,128)S(1)} all-reduce(f32[64,64]{0,1:T(8,128)S(1)} %psum.78), channel_id=1, replica_groups=mesh['band'=2,'grid'=16] {'band'}, use_global_device_ids=true, to_apply=%region_13.17 | all-reduce | flops 4096 | bytes 32768 | tf_op jit(solution)/shard_map/psum | solution.py:102
  515.7 5.8 %cholesky.81 = f32[64,64]{1,0:T(8,128)S(1)} custom-call(f32[64,64]{1,0:T(8,128)S(1)} %fusion.136), custom_call_target="Cholesky" | custom-call | tf_op jit(solution)/shard_map/jit(cholesky)/cholesky | solution.py:72
  522.9 4.9 custom-call.9
  529.8 3.5 all-to-all-start.6
  534.5 5.3 all-to-all-done.6
  (105 shorter events, 39.9 us)
Async XLA Ops:
  0.6 235.6 %copy-start = (f32[64,64]{1,0:T(8,128)S(1)}, f32[64,64]{1,0:T(8,128)}, u32[]{:S(2)}) copy-start(f32[64,64]{1,0:T(8,128)} %param.19) | copy-start | bytes 49156
  2.6 12.9 %all-to-all-start = ((f32[32,8,4,128]{3,2,0,1:T(4,128)}), f32[32,8,4,128]{3,2,0,1:T(4,128)S(1)}, u32[]{:S(2)}, u32[]{:S(2)}) async-start(f32[32,8,4,128]{3,2,0,1:T(4,128)} %copy.51), calls=%async_computation | async-start | bytes 1048576 | tf_op jit(solution)/shard_map/all_to_all | solution.py:96
  6.8 95.6 %copy-start.9 = (f32[8,4]{0,1:T(4,128)S(1)}, f32[8,4]{0,1:T(4,128)}, u32[]{:S(2)}) copy-start(f32[8,4]{0,1:T(4,128)} %param.23) | copy-start | bytes 388
  6.8 95.7 %copy-start.8 = (s32[8,128]{1,0:T(8,128)S(1)}, s32[8,128]{1,0:T(8,128)}, u32[]{:S(2)}) copy-start(s32[8,128]{1,0:T(8,128)} %param.21) | copy-start | bytes 12292
  98.9 10.1 %all-to-all-start.1 = ((f32[64,4,4,128]{3,2,1,0:T(4,128)}), f32[64,4,4,128]{3,2,1,0:T(4,128)S(1)}, u32[]{:S(2)}, u32[]{:S(2)}) async-start(f32[64,4,4,128]{3,2,1,0:T(4,128)} %reshape.180), calls=%async_computation.1 | async-start | bytes 1048576 | tf_op jit(solution)/shard_map/all_to_all | solution.py:99
  110.0 3.6 collective-permute-start
  113.6 0.8 copy-start.3
  114.4 7.5 %copy-start.6 = (f32[8,4,128]{2,1,0:T(4,128)S(1)}, f32[8,4,128]{2,1,0:T(4,128)}, u32[]{:S(2)}) copy-start(f32[8,4,128]{2,1,0:T(4,128)} %param.22) | copy-start | bytes 49156
  131.1 10.2 %copy-start.5 = (f32[32,8,4,128]{3,2,1,0:T(4,128)S(1)}, f32[32,8,4,128]{3,2,1,0:T(4,128)}, u32[]{:S(2)}) copy-start(f32[32,8,4,128]{3,2,1,0:T(4,128)} %param.18) | copy-start | bytes 1572868
  135.7 16.5 %collective-permute-start.2 = (f32[32,6,4,128]{3,0,2,1:T(8,128)}, f32[32,6,4,128]{3,0,2,1:T(8,128)}, u32[]{:S(2)}, u32[]{:S(2)}) collective-permute-start(f32[32,6,4,128]{3,0,2,1:T(8,128)} %copy.92), channel_id=1, source_target_pairs={{0,1},{1,2},{2,3},{3,4},{4,5},{5,6},{6,7},{7,8},{8,9},{9,10},{10,1... | collective-permute-start | bytes 1179656 | tf_op jit(solution)/shard_map/ppermute | solution.py:36
  139.3 14.8 %collective-permute-start.1 = (f32[32,6,4,128]{3,0,2,1:T(8,128)}, f32[32,6,4,128]{3,0,2,1:T(8,128)}, u32[]{:S(2)}, u32[]{:S(2)}) collective-permute-start(f32[32,6,4,128]{3,0,2,1:T(8,128)} %get-tuple-element.40), channel_id=1, source_target_pairs={{0,1},{1,2},{2,3},{3,4},{4,5},{5,6},{6,7},{7,8},{8,9},{9,10},{10,1... | collective-permute-start | bytes 1179656 | tf_op jit(solution)/shard_map/ppermute | solution.py:25
  142.2 16.2 %all-to-all-start.3 = ((f32[32,8,4,128]{3,2,0,1:T(4,128)}), f32[32,8,4,128]{3,2,0,1:T(4,128)}, u32[]{:S(2)}, u32[]{:S(2)}) async-start(f32[32,8,4,128]{3,2,0,1:T(4,128)} %copy.66), calls=%async_computation.3 | async-start | bytes 1048576 | tf_op jit(solution)/shard_map/all_to_all | solution.py:96
  148.2 5.9 %copy-start.7 = (f32[8,4,128]{2,1,0:T(4,128)S(1)}, f32[8,4,128]{2,1,0:T(4,128)}, u32[]{:S(2)}) copy-start(f32[8,4,128]{2,1,0:T(4,128)} %param.20) | copy-start | bytes 49156
  158.4 11.2 %all-to-all-start.2 = ((f32[32,8,4,128]{3,0,2,1:T(8,128)}), f32[32,8,4,128]{3,0,2,1:T(8,128)S(1)}, u32[]{:S(2)}, u32[]{:S(2)}) async-start(f32[32,8,4,128]{3,0,2,1:T(8,128)} %fusion.51), calls=%async_computation.2 | async-start | bytes 1048576 | tf_op jit(solution)/shard_map/all_to_all | solution.py:96
  316.6 9.4 %copy-start.1 = (f32[64,2048]{1,0:T(8,128)}, f32[64,2048]{1,0:T(8,128)S(1)}, u32[]{:S(2)}) copy-start(f32[64,2048]{1,0:T(8,128)S(1)} %fusion.147) | copy-start | bytes 1572868
  326.9 3.6 collective-permute-start.3
  330.5 0.7 copy-start.4
  352.6 11.3 %collective-permute-start.5 = (f32[32,6,4,128]{3,0,2,1:T(8,128)}, f32[32,6,4,128]{3,0,2,1:T(8,128)}, u32[]{:S(2)}, u32[]{:S(2)}) collective-permute-start(f32[32,6,4,128]{3,0,2,1:T(8,128)} %copy.95), channel_id=1, source_target_pairs={{0,1},{1,2},{2,3},{3,4},{4,5},{5,6},{6,7},{7,8},{8,9},{9,10},{10,1... | collective-permute-start | bytes 1179656 | tf_op jit(solution)/shard_map/ppermute | solution.py:36
  356.2 9.7 %collective-permute-start.4 = (f32[32,6,4,128]{3,0,2,1:T(8,128)}, f32[32,6,4,128]{3,0,2,1:T(8,128)}, u32[]{:S(2)}, u32[]{:S(2)}) collective-permute-start(f32[32,6,4,128]{3,0,2,1:T(8,128)} %get-tuple-element.38), channel_id=1, source_target_pairs={{0,1},{1,2},{2,3},{3,4},{4,5},{5,6},{6,7},{7,8},{8,9},{9,10},{10,1... | collective-permute-start | bytes 1179656 | tf_op jit(solution)/shard_map/ppermute | solution.py:25
  363.9 18.3 %copy-start.2 = (f32[64,2048]{1,0:T(8,128)S(1)}, f32[64,2048]{1,0:T(8,128)}, u32[]{:S(2)}) copy-start(f32[64,2048]{1,0:T(8,128)} %copy-done.1) | copy-start | bytes 1572868
  370.4 11.3 %all-to-all-start.5 = ((f32[32,8,4,128]{3,0,2,1:T(8,128)}), f32[32,8,4,128]{3,0,2,1:T(8,128)S(1)}, u32[]{:S(2)}, u32[]{:S(2)}) async-start(f32[32,8,4,128]{3,0,2,1:T(8,128)} %fusion.16), calls=%async_computation.5 | async-start | bytes 1048576 | tf_op jit(solution)/shard_map/all_to_all | solution.py:96
  529.8 10.1 %all-to-all-start.6 = ((f32[64,4,4,128]{3,2,1,0:T(4,128)}), f32[64,4,4,128]{3,2,1,0:T(4,128)S(1)}, u32[]{:S(2)}, u32[]{:S(2)}) async-start(f32[64,4,4,128]{3,2,1,0:T(4,128)} %reshape.195), calls=%async_computation.6 | async-start | bytes 1048576 | tf_op jit(solution)/shard_map/all_to_all | solution.py:99
